TPU v7x, 128 devices: a whole 4x4x4 slice. The times are simulated.
128 devices in a mesh: term: 32 (over y_lo, x, z), pair: 4 (over y_hi, core).
Axes of the slice: x: 4, y: 4 (y_hi: 2, y_lo: 2; y = y_hi * 2 + y_lo), z: 4, core: 2. Of those that a mesh axis runs over, the one named last changes fastest.
Arguments:
- core_rows: bfloat16 [12288, 256], P(('term', 'pair')), may hold values from -0.25 to 0.25
- norm_ops: bfloat16 [2048, 512, 512], P(('term', 'pair')), may hold values from -6 to 6
- norm_sectors: int32 [2048, 2], P(('term', 'pair')), may hold values from 0 to 23
- comp_ops: bfloat16 [2048, 512, 512], P(('term', 'pair')), may hold values from -1.5 to 1.5
- comp_sectors: int32 [2048, 2], P(('term', 'pair')), may hold values from 0 to 23
- comp_group: int32 [2048, 1], P(('term', 'pair')), may hold values from 0 to 3; in each aligned block of 16 rows (0 to 15, 16 to 31, ...) at most 8 rows name the same one
- comp_slot: int32 [2048], P(('term', 'pair')), may hold values from 0 to 31
Outputs:
- normal_rotated: bfloat16 [2048, 256, 256], P(('term', 'pair'))
- comp_rotated: bfloat16 [4, 32, 256, 256], P('pair', 'term')
Inputs may be any that keep to these rules, and one draw needn't show every extreme that they name: `comp_group`: among the complementary tiles of one device (aligned blocks of 16 rows), at most 8 name the same owner group, a bound that some block reaches of them.
All inputs are finite; a program needn't handle non-finite values.
Results may differ from a plain program's by a relative error of at most 0.017.
Values may be sent and summed in bfloat16 or wider, within the bound.
No kernel may reach another device: no remote copies, remote signals or barrier semaphores. Data moves between devices by JAX's collectives and lax.ppermute only.
A program may use at most 128 MiB of HBM per device.

v0:
```python
import jax
import jax.numpy as jnp
from jax import lax
from jax.sharding import PartitionSpec as P

PAIR_DEV = 1


def rotate_tiles(core_tiles, op_tiles, sector_ids):
    left_rot = core_tiles[sector_ids[:, 0]]
    right_rot = core_tiles[sector_ids[:, 1]]
    half_rotated = jnp.einsum(
        "nab,nbc->nac", op_tiles, right_rot, preferred_element_type=jnp.float32
    ).astype(jnp.bfloat16)
    return jnp.einsum("nba,nbc->nac", left_rot, half_rotated, preferred_element_type=jnp.float32)


def on_device(core_rows, norm_ops, norm_sectors, comp_ops, comp_sectors, comp_group, comp_slot):
    tile_width = core_rows.shape[1]
    row_width = norm_ops.shape[1]
    gathered = lax.all_gather(core_rows, ("term", "pair"), axis=0, tiled=True)
    core_tiles = gathered.reshape(-1, row_width, tile_width)
    normal_rotated = rotate_tiles(core_tiles, norm_ops, norm_sectors).astype(jnp.bfloat16)
    groups = lax.axis_size("pair")
    term_count = lax.axis_size("term")
    comp_count = comp_ops.shape[0]
    capacity = comp_count // 2
    owned_slots = PAIR_DEV * term_count
    group_ids = comp_group[:, 0]
    member = (group_ids[:, None] == jnp.arange(groups, dtype=jnp.int32)[None, :]).astype(jnp.int32)
    before = jnp.cumsum(member, axis=0) - member
    target = group_ids * capacity + jnp.sum(before * member, axis=1)
    dispatch = target[None, :] == jnp.arange(groups * capacity, dtype=jnp.int32)[:, None]
    dispatch_bf = dispatch.astype(jnp.bfloat16)
    slots_out = (jnp.sum(jnp.where(dispatch, comp_slot[None, :] + 1, 0), axis=1) - 1).reshape(
        groups, capacity
    )
    rotated = (
        rotate_tiles(core_tiles, comp_ops, comp_sectors)
        .astype(jnp.bfloat16)
        .reshape(comp_count, -1)
    )
    outgoing = jnp.dot(dispatch_bf, rotated, preferred_element_type=jnp.float32)
    outgoing = outgoing.astype(jnp.bfloat16).reshape(groups, capacity, tile_width * tile_width)
    received, slots_in = (
        lax.all_to_all(outgoing, "pair", split_axis=0, concat_axis=0, tiled=True),
        lax.all_to_all(slots_out, "pair", split_axis=0, concat_axis=0, tiled=True),
    )
    select = (slots_in.reshape(1, -1) == jnp.arange(owned_slots, dtype=jnp.int32)[:, None]).astype(
        jnp.bfloat16
    )
    partial_value = jnp.dot(
        select, received.reshape(-1, tile_width * tile_width), preferred_element_type=jnp.float32
    )
    partial_bf = partial_value.astype(jnp.bfloat16)
    owned_sums = lax.psum_scatter(
        partial_bf.astype(jnp.float32).astype(jnp.bfloat16), "term", scatter_dimension=0, tiled=True
    )
    comp_rotated = owned_sums.reshape(1, PAIR_DEV, tile_width, tile_width)
    return (normal_rotated, comp_rotated)


def solution(mesh):
    return jax.shard_map(
        on_device,
        mesh=mesh,
        in_specs=(
            P(("term", "pair"), None),
            P(("term", "pair"), None, None),
            P(("term", "pair"), None),
            P(("term", "pair"), None, None),
            P(("term", "pair"), None),
            P(("term", "pair"), None),
            P(("term", "pair")),
        ),
        out_specs=(P(("term", "pair"), None, None), P("pair", "term", None, None)),
        check_vma=False,
    )
```

profile of v0, /device:TPU:0, one launch (start us, length us, event | category | flops | bytes accessed | tf_op | source)
XLA Modules:
  0.0 625.8 jit_solution(5890029725378413766)
XLA Ops:
  7.2 0.0 all-gather.2.cloned.1.call-start
  7.2 0.7 all-gather.2.cloned.1.call-update
  7.9 0.7 fusion.17
  8.7 0.8 select_reduce_fusion.1
  9.5 0.7 multiply_add_fusion
  10.2 0.1 select_reduce_fusion
  10.3 0.7 sub.11
  10.9 4.6 all-to-all-start
  15.5 0.8 fusion.22
  16.3 195.9 %all-gather.2.cloned.1.call-done = bf16[12288,256]{1,0:T(8,128)(2,1)} async-done(((bf16[96,256]{1,0:T(8,128)(2,1)}), bf16[12288,256]{1,0:T(8,128)(2,1)}) %all-gather.2.cloned.1.call-update) | async-done | bytes 6291472 | tf_op jit(solution)/shard_map/all_gather | solution.py:21
  212.2 5.6 gather_fusion.2
  217.8 5.7 gather_fusion.3
  223.5 7.8 %fusion.13 = bf16[16,256,256]{2,1,0:T(8,128)(2,1)S(1)} fusion(bf16[16,512,256]{2,1,0:T(8,128)(2,1)} %gather_fusion.2, bf16[16,512,256]{2,1,0:T(8,128)(2,1)} %gather_fusion.3, bf16[16,512,512]{2,1,0:T(8,128)(2,1)} %param.10), kind=kOutput, calls=%fused_computation.15 | convolution fusion | flops 3224371200 | bytes 18874368 | tf_op jit(solution)/shard_map/nba,nbc->nac/dot_general | solution.py:15
  231.3 1.2 copy.25
  232.5 3.4 fusion
  235.8 0.0 all-to-all-done
  235.9 4.8 all-to-all-start.1
  240.7 0.0 all-reduce.3.cloned.1.call-start
  240.8 0.5 broadcast.80
  241.3 0.7 reduce.5
  241.9 0.1 eq.47
  242.0 48.4 %all-to-all-done.1 = bf16[4,8,65536]{2,1,0:T(8,128)(2,1)} async-done(((bf16[4,8,65536]{2,1,0:T(8,128)(2,1)}), bf16[4,8,65536]{2,1,0:T(8,128)(2,1)}, u32[]{:S(2)}, u32[]{:S(2)}) %all-to-all-start.1) | async-done | bytes 4194336 | tf_op jit(solution)/shard_map/all_to_all | solution.py:46
  290.4 5.5 convolution_convert_fusion
  295.9 0.0 copy-start.1
  295.9 0.0 copy-start
  295.9 0.0 all-reduce.3.cloned.1.call-update
  295.9 0.6 copy-done.1
  296.5 0.6 dynamic-slice
  297.1 0.0 copy-done
  297.1 5.6 gather_fusion.1
  302.7 5.6 gather_fusion
  308.3 8.8 %fusion.10 = bf16[16,256,256]{2,1,0:T(8,128)(2,1)} fusion(bf16[16,512,256]{2,1,0:T(8,128)(2,1)} %gather_fusion, bf16[16,512,256]{2,1,0:T(8,128)(2,1)} %gather_fusion.1, bf16[16,512,512]{2,1,0:T(8,128)(2,1)} %param.8), kind=kOutput, calls=%fused_computation.14 | convolution fusion | flops 3224371200 | bytes 18874368 | tf_op jit(solution)/shard_map/nba,nbc->nac/dot_general | solution.py:15
  317.2 298.4 %all-reduce.3.cloned.1.call-done = bf16[32,65536]{1,0:T(8,128)(2,1)} async-done(((bf16[32,65536]{1,0:T(8,128)(2,1)}), bf16[32,65536]{1,0:T(8,128)(2,1)}) %all-reduce.3.cloned.1.call-update) | async-done | bytes 4194320
  615.6 2.7 dynamic-slice_reduce_fusion
  618.3 0.7 reshape.52
  (5 shorter events, 0.1 us)
Async XLA Ops:
  7.2 205.0 %all-gather.2.cloned.1.call-start = ((), (), s32[]{:S(2)}) async-start(), calls=%async_computation.2 | async-start | bytes 6340608 | tf_op jit(solution)/shard_map/all_gather | solution.py:21
  10.9 224.9 %all-to-all-start = ((s32[4,1,8]{2,1,0:T(1,128)}), s32[4,1,8]{2,1,0:T(1,128)S(1)}, u32[]{:S(2)}, u32[]{:S(2)}) async-start(s32[4,1,8]{2,1,0:T(1,128)} %bitcast.4), calls=%async_computation | async-start | bytes 4096 | tf_op jit(solution)/shard_map/all_to_all | solution.py:47
  235.9 54.6 %all-to-all-start.1 = ((bf16[4,8,65536]{2,1,0:T(8,128)(2,1)}), bf16[4,8,65536]{2,1,0:T(8,128)(2,1)}, u32[]{:S(2)}, u32[]{:S(2)}) async-start(bf16[4,8,65536]{2,1,0:T(8,128)(2,1)} %fusion), calls=%async_computation.1 | async-start | bytes 8388608 | tf_op jit(solution)/shard_map/all_to_all | solution.py:46
  240.7 374.9 %all-reduce.3.cloned.1.call-start = ((), (), s32[]{:S(2)}) async-start(), calls=%async_computation.3 | async-start | bytes 8388608
  295.9 0.7 copy-start.1
  295.9 1.2 copy-start
Sparse Core Ops, SparseCore 0:
  9.7 202.4 all-gather.1
  296.0 319.5 all-reduce.2
where the time goes:
time: 626 us
  waiting for transfers between devices  543 us (87%)
  local copies, waits for them, and re-layouts  29.5 us (5%)
  matrix products  25.5 us (4%)
  between operations  14.1 us (2%)
  starting transfers between devices  9.5 us (2%)
    unnamed x3, waiting for transfers between devices  299 us
    all_gather x1, waiting for transfers between devices, on_device(): gathered = lax.all_gather(core_rows, ('term', 'pair'), axis=0, tiled=True)  196 us
    all_to_all x1, waiting for transfers between devices, on_device(): lax.all_to_all(outgoing, 'pair', split_axis=0, concat_axis=0, tiled=True)  48.4 us
    dot_general x2, matrix products, rotate_tiles(): jnp.einsum('nba,nbc->nac', left_rot, half_rotated, preferred_element_type...  16.7 us
  transfers between devices with their start and end apart: 4, of which 3 were waited for; matrix products, arithmetic and copies ran while one was open for 8% of the time, Pallas kernels for 0%

commit v1 on v0

v1 whole, which is shorter than its diff:
```python
import functools

import jax
import jax.numpy as jnp
from jax import lax
from jax.experimental import pallas as pl
from jax.experimental.pallas import tpu as pltpu
from jax.sharding import Mesh
from jax.sharding import PartitionSpec as P

AXES = ("ylo", "x", "z", "yhi", "core")
SIZES = (2, 4, 4, 2, 2)
TERM = ("ylo", "x", "z")
CHIPS = ("ylo", "x", "z", "yhi")
CHUNKS = 1


def rotate_kernel(chunks, sectors, place, core, own_ref, other_ref, op_ref, out_ref, u_ref, sem):
    step = pl.program_id(0)
    blocks, block_rows, _ = own_ref.shape

    @pl.when(step == 0)
    def _():
        mine = core[0]

        def copies(j):
            first = pl.multiple_of((2 * j + mine) * block_rows, 32)
            second = pl.multiple_of((2 * j + 1 - mine) * block_rows, 32)
            return (
                pltpu.make_async_copy(own_ref.at[j], u_ref.at[pl.ds(first, block_rows)], sem),
                pltpu.make_async_copy(other_ref.at[j], u_ref.at[pl.ds(second, block_rows)], sem),
            )

        @pl.loop(0, blocks)
        def _(j):
            for copy in copies(j):
                copy.start()

        @pl.loop(0, blocks)
        def _(j):
            for copy in copies(j):
                copy.wait()

    depth = op_ref.shape[1]
    left = u_ref[pl.ds(pl.multiple_of(sectors[step, 0] * depth, depth), depth), :]
    right = u_ref[pl.ds(pl.multiple_of(sectors[step, 1] * depth, depth), depth), :]
    half = jnp.dot(op_ref[0], right, preferred_element_type=jnp.float32).astype(jnp.bfloat16)
    full = lax.dot_general(
        left, half, (((0,), (0,)), ((), ())), preferred_element_type=jnp.float32
    ).astype(jnp.bfloat16)
    rows = full.shape[0] // chunks
    for k in range(chunks):
        out_ref[k, 0] = full[k * rows : (k + 1) * rows]


def rotate(own, other, core, ops, sectors, place, slots, chunks):
    count, depth, _ = ops.shape
    width = own.shape[2]
    rows = width // chunks
    return pl.pallas_call(
        functools.partial(rotate_kernel, chunks),
        out_shape=jax.ShapeDtypeStruct((chunks, slots, rows, width), jnp.bfloat16),
        grid_spec=pltpu.PrefetchScalarGridSpec(
            num_scalar_prefetch=3,
            grid=(count,),
            in_specs=[
                pl.BlockSpec(memory_space=pl.ANY),
                pl.BlockSpec(memory_space=pl.ANY),
                pl.BlockSpec((1, depth, depth), lambda i, s, p, c: (i, 0, 0)),
            ],
            out_specs=pl.BlockSpec((chunks, 1, rows, width), lambda i, s, p, c: (0, p[i], 0, 0)),
            scratch_shapes=[
                pltpu.VMEM((2 * own.shape[0] * own.shape[1], width), jnp.bfloat16),
                pltpu.SemaphoreType.DMA,
            ],
        ),
        cost_estimate=pl.CostEstimate(
            flops=count * 2 * depth * width * (depth + width),
            bytes_accessed=2 * (count * depth * depth + 2 * own.size + count * width * width),
            transcendentals=0,
        ),
    )(sectors, place, core, own, other, ops)


def combine_kernel(order, start, tiles_ref, out_ref):
    slots, rows, width = out_ref.shape
    piece = 64 if rows >= 64 else rows

    @pl.loop(0, slots)
    def _(p):
        for r in range(0, rows, piece):

            def add(j, total):
                return total + tiles_ref[order[j], r : r + piece, :].astype(jnp.float32)

            total = lax.fori_loop(
                start[p], start[p + 1], add, jnp.zeros((piece, width), jnp.float32)
            )
            out_ref[p, r : r + piece, :] = total.astype(jnp.bfloat16)


def combine(tiles, order, start, slots):
    _, rows, width = tiles.shape
    return pl.pallas_call(
        combine_kernel,
        out_shape=jax.ShapeDtypeStruct((slots, rows, width), jnp.bfloat16),
        grid_spec=pltpu.PrefetchScalarGridSpec(
            num_scalar_prefetch=2,
            grid=(1,),
            in_specs=[pl.BlockSpec(tiles.shape, lambda i, o, s: (0, 0, 0))],
            out_specs=pl.BlockSpec((slots, rows, width), lambda i, o, s: (0, 0, 0)),
        ),
        cost_estimate=pl.CostEstimate(
            flops=tiles.size, bytes_accessed=4 * tiles.size, transcendentals=0
        ),
    )(order, start, tiles)


def exchange(x, axes):
    return lax.all_to_all(x, axes, split_axis=0, concat_axis=0, tiled=True)


def on_device(core_rows, norm_ops, norm_sectors, comp_ops, comp_sectors, comp_group, comp_slot):
    width = core_rows.shape[1]
    count = comp_ops.shape[0]
    groups = lax.axis_size("yhi") * lax.axis_size("core")
    terms = lax.axis_size(TERM)
    chips = lax.axis_size(CHIPS)
    capacity = count // 2

    own = exchange(jnp.broadcast_to(core_rows[None], (chips, *core_rows.shape)), CHIPS)
    other = lax.ppermute(own, "core", [(0, 1), (1, 0)])
    core = lax.axis_index("core").reshape(1).astype(jnp.int32)

    group = comp_group[:, 0]
    member = group[:, None] == jnp.arange(groups, dtype=jnp.int32)[None, :]
    earlier = jnp.arange(count)[:, None] > jnp.arange(count)[None, :]
    rank = jnp.sum((group[:, None] == group[None, :]) & earlier, axis=1, dtype=jnp.int32)
    place = group * capacity + rank
    sent = groups * capacity
    dispatch = place[None, :] == jnp.arange(sent, dtype=jnp.int32)[:, None]
    slots_out = jnp.sum(jnp.where(dispatch, comp_slot[None, :] + 1, 0), axis=1) - 1
    slots_in = exchange(slots_out.reshape(groups, capacity), ("yhi", "core")).reshape(sent)
    key = jnp.where(slots_in < 0, terms, slots_in)
    j = jnp.arange(sent, dtype=jnp.int32)
    before = (key[None, :] < key[:, None]) | ((key[None, :] == key[:, None]) & (j[None, :] < j[:, None]))
    at = jnp.sum(before, axis=1, dtype=jnp.int32)
    order = jnp.sum(jnp.where(at[None, :] == j[:, None], j[None, :], 0), axis=1, dtype=jnp.int32)
    start = jnp.sum(
        key[None, :] < jnp.arange(terms + 1, dtype=jnp.int32)[:, None], axis=1, dtype=jnp.int32
    )

    outgoing = rotate(own, other, core, comp_ops, comp_sectors, place, sent, CHUNKS)
    pieces = []
    for k in range(CHUNKS):
        received = exchange(outgoing[k], ("yhi", "core"))
        partial = combine(received, order, start, terms)
        parts = exchange(partial, TERM)
        pieces.append(jnp.sum(parts.astype(jnp.float32), axis=0).astype(jnp.bfloat16))
    comp_rotated = jnp.concatenate(pieces, axis=0).reshape(1, 1, width, width)

    ids = jnp.arange(norm_ops.shape[0], dtype=jnp.int32)
    normal = rotate(own, other, core, norm_ops, norm_sectors, ids, norm_ops.shape[0], 1)
    return normal.reshape(-1, width, width), comp_rotated


def solution(mesh):
    cut = Mesh(mesh.devices.reshape(SIZES), AXES)
    every = AXES
    return jax.shard_map(
        on_device,
        mesh=cut,
        in_specs=(
            P(every, None),
            P(every, None, None),
            P(every, None),
            P(every, None, None),
            P(every, None),
            P(every, None),
            P(every),
        ),
        out_specs=(P(every, None, None), P(("yhi", "core"), TERM, None, None)),
        check_vma=False,
    )
```

time: 626 us -> 206 us (0.33)
  waiting for transfers between devices: 543 us -> 84.3 us
  blocking collectives: 0 us -> 52.4 us
  Pallas kernels: 0 us -> 43.1 us
  matrix products: 25.5 us -> 0 us
  local copies, waits for them, and re-layouts: 29.5 us -> 4.71 us
  between operations: 14.1 us -> 0.77 us
    unnamed x3 -> x0, waiting for transfers between devices: 299 us -> none
    all_gather x1 -> x0, waiting for transfers between devices: 196 us -> none  [on_device(): gathered = lax.all_gather(core_rows, ('term', 'pair'), axis=0, tiled=True)]
    all_to_all x0 -> x1, blocking collectives: none -> 52.4 us  [exchange(): return lax.all_to_all(x, axes, split_axis=0, concat_axis=0, tiled=True)]
    pallas_call x0 -> x3, Pallas kernels: none -> 43.1 us  [the longest x2 36.7 us: rotate(): pl.pallas_call(functools.partial(rotate_kernel, chunks), out_shape=jax.Sh...]
    all_to_all x2 -> x3, waiting for transfers between devices: 48.4 us -> 83.7 us  [exchange(): return lax.all_to_all(x, axes, split_axis=0, concat_axis=0, tiled=True)]
    dot_general x4 -> x0, matrix products: 25.5 us -> none  [the longest x2 16.7 us: rotate_tiles(): jnp.einsum('nba,nbc->nac', left_rot, half_rotated, preferred_element_type...]
    gather x4 -> x0, local copies, waits for them, and re-layouts: 22.5 us -> none  [the longest x2 11.3 us: rotate_tiles(): right_rot = core_tiles[sector_ids[:, 1]]]
    all_to_all x2 -> x3, starting transfers between devices: 9.42 us -> 13.1 us  [exchange(): return lax.all_to_all(x, axes, split_axis=0, concat_axis=0, tiled=True)]
  transfers between devices with their start and end apart: 4 -> 4, of which waited for: 3 -> 3; matrix products, arithmetic and copies ran while one was open for 8% -> 3% of each run, Pallas kernels for 0% -> 18%
where the time goes in v1:
time: 206 us; the launch traced here: 204 us
  waiting for transfers between devices  84.3 us (41%)
  blocking collectives  52.4 us (25%)
  Pallas kernels  43.1 us (21%)
  starting transfers between devices  13.1 us (6%)
  other arithmetic  5.83 us (3%)
  local copies, waits for them, and re-layouts  4.71 us (2%)
    all_to_all x3, waiting for transfers between devices, exchange(): return lax.all_to_all(x, axes, split_axis=0, concat_axis=0, tiled=True)  83.7 us
    all_to_all x1, blocking collectives, exchange(): return lax.all_to_all(x, axes, split_axis=0, concat_axis=0, tiled=True)  52.4 us
    pallas_call x2, Pallas kernels, rotate(): pl.pallas_call(functools.partial(rotate_kernel, chunks), out_shape=jax.Sh...  36.7 us
    all_to_all x3, starting transfers between devices, exchange(): return lax.all_to_all(x, axes, split_axis=0, concat_axis=0, tiled=True)  13.1 us
    pallas_call x1, Pallas kernels, combine(): pl.pallas_call(combine_kernel, out_shape=jax.ShapeDtypeStruct((slots, row...  6.4 us
  transfers between devices with their start and end apart: 4, of which 3 were waited for; matrix products, arithmetic and copies ran while one was open for 3% of the time, Pallas kernels for 18%

profile of v1, /device:TPU:0, one launch (start us, length us, event | category | flops | bytes accessed | tf_op | source)
XLA Modules:
  0.0 204.2 jit_solution(13848249146296699040)
XLA Ops:
  0.6 0.0 copy-start.5
  0.6 0.0 copy-start.4
  0.7 0.0 copy-start.1
  0.7 1.2 broadcast_in_dim.24
  1.9 52.4 %all_to_all.21.own_ref = bf16[64,96,256]{2,1,0:T(8,128)(2,1)S(1)} all-to-all(bf16[64,96,256]{2,1,0:T(8,128)(2,1)S(1)} %broadcast_in_dim.24), channel_id=1, replica_groups=mesh['ylo'=2,'x'=4,'z'=4,'yhi'=2,'core'=2] {'ylo','x','z','yhi'}, dimensions={0} | all-to-all | bytes 6291456 | tf_op jit(solution)/shard_map/all_to_all | solution.py:120
  54.2 0.0 copy-start
  54.2 0.0 collective-permute-start
  54.2 0.0 copy-done.5
  54.2 0.2 convert_reduce_fusion.2
  54.4 0.0 copy-done.4
  54.4 0.0 copy-start.3
  54.5 0.1 select_reduce_fusion.1
  54.6 1.0 sub.7
  55.5 3.2 %all-to-all-start.1 = ((s32[4,1,8]{2,1,0:T(1,128)}), s32[4,1,8]{2,1,0:T(1,128)S(1)}, u32[]{:S(2)}, u32[]{:S(2)}) async-start(s32[4,1,8]{2,1,0:T(1,128)} %bitcast.3), calls=%async_computation.1 | async-start | bytes 4096 | tf_op jit(solution)/shard_map/all_to_all | solution.py:120
  58.7 0.0 copy-done.1
  58.7 0.7 copy.16.sectors
  59.4 0.6 collective-permute-done.other_ref
  60.0 0.0 copy-done
  60.0 0.0 copy-done.3
  60.0 18.4 %shard_map.87 = bf16[1,32,256,256]{3,2,1,0:T(8,128)(2,1)} custom-call(s32[16,2]{1,0:T(8,128)} %copy.16.sectors, s32[16]{0:T(128)} %copy-done.3, s32[1]{0:T(128)} %bitcast.core, bf16[64,96,256]{2,1,0:T(8,128)(2,1)} %copy-done, bf16[64,96,256]{2,1,0:T(8,128)(2,1)} %collective-permute-done.other_ref, bf16[16,512,512]{2,1,0:T(8,128)(2,1)} %op_ref.3), custom_call_target="tpu_custom_call" | custom-call | flops 3221225472 | bytes 16777216 | tf_op jit(solution)/shard_map/pallas_call | solution.py:60
  78.4 0.0 all-to-all-done.1
  78.4 4.9 %all-to-all-start.2 = ((bf16[32,256,256]{2,1,0:T(8,128)(2,1)}), bf16[32,256,256]{2,1,0:T(8,128)(2,1)}, u32[]{:S(2)}, u32[]{:S(2)}) async-start(bf16[32,256,256]{2,1,0:T(8,128)(2,1)} %bitcast.7), calls=%async_computation.2 | async-start | bytes 8388608 | tf_op jit(solution)/shard_map/all_to_all | solution.py:120
  83.3 0.5 broadcast.52
  83.8 0.7 reduce.4
  84.5 0.1 reshape.67
  84.5 0.2 convert_reduce_fusion.1
  84.7 0.6 select_reduce_fusion.order
  85.4 0.6 convert_reduce_fusion.start
  86.0 47.0 %all-to-all-done.2.tiles_ref = bf16[32,256,256]{2,1,0:T(8,128)(2,1)} async-done(((bf16[32,256,256]{2,1,0:T(8,128)(2,1)}), bf16[32,256,256]{2,1,0:T(8,128)(2,1)}, u32[]{:S(2)}, u32[]{:S(2)}) %all-to-all-start.2) | async-done | bytes 4194336 | tf_op jit(solution)/shard_map/all_to_all | solution.py:120
  133.0 6.4 %shard_map.88 = bf16[32,256,256]{2,1,0:T(8,128)(2,1)} custom-call(s32[32]{0:T(128)} %select_reduce_fusion.order, s32[33]{0:T(128)} %convert_reduce_fusion.start, bf16[32,256,256]{2,1,0:T(8,128)(2,1)} %all-to-all-done.2.tiles_ref), custom_call_target="tpu_custom_call" | custom-call | flops 2097152 | bytes 8388608 | tf_op jit(solution)/shard_map/pallas_call | solution.py:104
  139.4 0.0 copy-start.2
  139.4 5.0 %all-to-all-start.3 = ((bf16[32,256,256]{2,1,0:T(8,128)(2,1)}), bf16[32,256,256]{2,1,0:T(8,128)(2,1)}, u32[]{:S(2)}, u32[]{:S(2)}) async-start(bf16[32,256,256]{2,1,0:T(8,128)(2,1)} %shard_map.88), calls=%async_computation.3 | async-start | bytes 8388608 | tf_op jit(solution)/shard_map/all_to_all | solution.py:120
  144.4 0.0 copy-done.2
  144.4 0.7 copy.14.sectors
  145.1 0.6 iota.24.place
  145.7 18.3 %shard_map.86 = bf16[1,16,256,256]{3,2,1,0:T(8,128)(2,1)} custom-call(s32[16,2]{1,0:T(8,128)} %copy.14.sectors, s32[16]{0:T(128)} %iota.24.place, s32[1]{0:T(128)} %bitcast.core, bf16[64,96,256]{2,1,0:T(8,128)(2,1)} %copy-done, bf16[64,96,256]{2,1,0:T(8,128)(2,1)} %collective-permute-done.other_ref, bf16[16,512,512]{2,1,0:T(8,128)(2,1)} %op_ref.2), custom_call_target="tpu_custom_call" | custom-call | flops 3221225472 | bytes 16777216 | tf_op jit(solution)/shard_map/pallas_call | solution.py:60
  164.0 36.7 %all-to-all-done.3 = bf16[32,256,256]{2,1,0:T(8,128)(2,1)} async-done(((bf16[32,256,256]{2,1,0:T(8,128)(2,1)}), bf16[32,256,256]{2,1,0:T(8,128)(2,1)}, u32[]{:S(2)}, u32[]{:S(2)}) %all-to-all-start.3) | async-done | bytes 4194336 | tf_op jit(solution)/shard_map/all_to_all | solution.py:120
  200.7 3.5 %reduce_sum.62 = bf16[256,256]{1,0:T(8,128)(2,1)} reduce(bf16[32,256,256]{2,1,0:T(8,128)(2,1)} %all-to-all-done.3, bf16[]{:T(256)} %constant.18.clone.1), dimensions={0}, to_apply=%region_5.6 | reduce | flops 2031616 | bytes 4325378 | tf_op jit(solution)/shard_map/reduce_sum | solution.py:159
  (4 shorter events, 0.0 us)
Async XLA Ops:
  0.6 53.6 %copy-start.5 = (s32[16,1]{0,1:T(1,128)S(1)}, s32[16,1]{0,1:T(1,128)}, u32[]{:S(2)}) copy-start(s32[16,1]{0,1:T(1,128)} %param.12) | copy-start | bytes 196
  0.6 53.8 %copy-start.4 = (s32[16]{0:T(128)S(1)}, s32[16]{0:T(128)}, u32[]{:S(2)}) copy-start(s32[16]{0:T(128)} %param.13) | copy-start | bytes 196
  0.7 58.1 %copy-start.1 = (s32[16,2]{0,1:T(2,128)S(1)}, s32[16,2]{0,1:T(2,128)}, u32[]{:S(2)}) copy-start(s32[16,2]{0,1:T(2,128)} %param.11) | copy-start | bytes 388
  54.2 5.8 %copy-start = (bf16[64,96,256]{2,1,0:T(8,128)(2,1)}, bf16[64,96,256]{2,1,0:T(8,128)(2,1)S(1)}, u32[]{:S(2)}) copy-start(bf16[64,96,256]{2,1,0:T(8,128)(2,1)S(1)} %all_to_all.21.own_ref) | copy-start | bytes 9437188
  54.2 5.8 %collective-permute-start = (bf16[64,96,256]{2,1,0:T(8,128)(2,1)S(1)}, bf16[64,96,256]{2,1,0:T(8,128)(2,1)}, u32[]{:S(2)}, u32[]{:S(2)}) collective-permute-start(bf16[64,96,256]{2,1,0:T(8,128)(2,1)S(1)} %all_to_all.21.own_ref), channel_id=1, source_target_pairs={{0,1},{1,0},{2,3},{3,2},{4,5},{5,4},{6,7},{7,6},{8,9},{9,8},{10,11... | collective-permute-start | bytes 9437192 | tf_op jit(solution)/shard_map/ppermute | solution.py:132
  54.4 5.6 %copy-start.3 = (s32[16]{0:T(128)}, s32[16]{0:T(128)S(1)}, u32[]{:S(2)}) copy-start(s32[16]{0:T(128)S(1)} %multiply_add_fusion.place) | copy-start | bytes 196
  55.5 22.9 %all-to-all-start.1 = ((s32[4,1,8]{2,1,0:T(1,128)}), s32[4,1,8]{2,1,0:T(1,128)S(1)}, u32[]{:S(2)}, u32[]{:S(2)}) async-start(s32[4,1,8]{2,1,0:T(1,128)} %bitcast.3), calls=%async_computation.1 | async-start | bytes 4096 | tf_op jit(solution)/shard_map/all_to_all | solution.py:120
  78.4 54.6 %all-to-all-start.2 = ((bf16[32,256,256]{2,1,0:T(8,128)(2,1)}), bf16[32,256,256]{2,1,0:T(8,128)(2,1)}, u32[]{:S(2)}, u32[]{:S(2)}) async-start(bf16[32,256,256]{2,1,0:T(8,128)(2,1)} %bitcast.7), calls=%async_computation.2 | async-start | bytes 8388608 | tf_op jit(solution)/shard_map/all_to_all | solution.py:120
  139.4 5.0 %copy-start.2 = (s32[16,2]{0,1:T(2,128)S(1)}, s32[16,2]{0,1:T(2,128)}, u32[]{:S(2)}) copy-start(s32[16,2]{0,1:T(2,128)} %param.9) | copy-start | bytes 388
  139.4 61.4 %all-to-all-start.3 = ((bf16[32,256,256]{2,1,0:T(8,128)(2,1)}), bf16[32,256,256]{2,1,0:T(8,128)(2,1)}, u32[]{:S(2)}, u32[]{:S(2)}) async-start(bf16[32,256,256]{2,1,0:T(8,128)(2,1)} %shard_map.88), calls=%async_computation.3 | async-start | bytes 8388608 | tf_op jit(solution)/shard_map/all_to_all | solution.py:120
